TPU v7x, 256 devices: a whole 4x4x8 slice. The times are simulated.
256 devices in a mesh: gx: 4 (over y), gy: 8 (over x, core), gz: 8 (over z).
Axes of the slice: x: 4, y: 4, z: 8, core: 2. Of those that a mesh axis runs over, the one named last changes fastest.
Arguments:
- basis: bfloat16 [8, 3, 64, 1024, 128], P('gx', None, 'gy', 'gz'), may hold values from -4.8 to 4.8
- modal_now: bfloat16 [128, 8], replicated, may hold values from -0.5 to 0.5
- modal_prev: bfloat16 [128, 8], replicated, may hold values from -0.5 to 0.5
- material_ids: int32 [8, 64, 1024], P('gx', 'gy', 'gz'), may hold values from 0 to 3
- moduli: float32 [3, 4], replicated, may hold values from 0.4 to 1.6
- drive_mask: int32 [8, 8, 64, 1024], P(None, 'gx', 'gy', 'gz'), may hold values 0 or 1
- drive: float32 [3, 8], replicated, may hold values from -8 to 8
Outputs:
- displacement: float32 [3, 8, 8, 64, 1024], P(None, None, 'gx', 'gy', 'gz')
- modes: float32 [3, 8, 8, 64, 1024], P(None, None, 'gx', 'gy', 'gz')
- coefficients: float32 [4, 2, 128, 8], replicated
- rfactor: float32 [4, 8, 8], replicated
All inputs are finite; a program needn't handle non-finite values. No bound on the sum of `drive_mask` on one device may be relied on, other than what follows from the above.
Results may differ from a plain program's by a relative error of at most 0.0008.
The roundings to bfloat16 on the way count: a program that leaves them out, or rounds other values in their place, can miss the bound.
Values sent between devices are 32-bit elements; how exact they have to be, the bound alone decides.
No kernel may reach another device: no remote copies, remote signals or barrier semaphores. Data moves between devices by JAX's collectives and lax.ppermute only.
A program may use at most 128 MiB of HBM per device.

v0:
```python
import jax
import jax.numpy as jnp
from jax import lax
from jax.sharding import PartitionSpec as P

STEPS = 4
step_squared = 0.1
ramp_steps = 4.0


def padded_2(block, sides, width):
    for axis, dim in sides:
        count = lax.axis_size(axis)
        forward = [(i, i + 1) for i in range(count - 1)]
        backward = [(target, source) for source, target in forward]
        low = lax.ppermute(
            lax.slice_in_dim(block, block.shape[dim] - width, None, axis=dim), axis, forward
        )
        high = lax.ppermute(lax.slice_in_dim(block, 0, width, axis=dim), axis, backward)
        block = jnp.concatenate([low, block, high], axis=dim)
    return block


def interior(array, direction_axis, offset):
    base_axis = array.ndim - 3
    result = array
    for axis_index in range(3):
        extent = array.shape[base_axis + axis_index]
        begin = offset if axis_index == direction_axis else 1
        result = lax.slice_in_dim(result, begin, extent - 2 + begin, axis=base_axis + axis_index)
    return result


def stiffness(field, material_props):
    component_rows = []
    for component in range(3):
        center = interior(field[component], 0, 1)
        accumulated = jnp.zeros_like(center)
        for direction_axis in range(3):
            modulus = material_props[0] if component == direction_axis else material_props[1]
            center_modulus = interior(modulus, 0, 1)
            for offset in (0, 2):
                coupling = 0.5 * (center_modulus + interior(modulus, direction_axis, offset))
                accumulated = accumulated + coupling * (
                    center - interior(field[component], direction_axis, offset)
                )
        component_rows.append(accumulated)
    return jnp.stack(component_rows)


def lookup(material_ids, moduli):
    levels = jnp.arange(moduli.shape[1], dtype=jnp.int32)
    onehot = (material_ids[None] == levels[:, None, None, None]).astype(jnp.float32)
    return jnp.einsum("mxyz,pm->pxyz", onehot, moduli, precision=lax.Precision.HIGHEST)


def expand(basis, coefficient):
    return jnp.einsum("xcyzk,kj->cjxyz", basis, coefficient, preferred_element_type=jnp.float32)


def project(basis, field):
    return jnp.einsum("xcyzk,cjxyz->kj", basis, field, preferred_element_type=jnp.float32)


def apply_inverse(block, lower_factor):
    identity_block = jnp.eye(lower_factor.shape[0], dtype=jnp.float32)
    lower_inverse = jax.scipy.linalg.solve_triangular(lower_factor, identity_block, lower=True)
    return jnp.einsum("cixyz,ji->cjxyz", block, lower_inverse, precision=lax.Precision.HIGHEST)


def local_gram(block):
    return jnp.einsum("cixyz,cjxyz->ij", block, block, precision=lax.Precision.HIGHEST)


def orthonormalize(following, basis, dof_weight):
    highest = lax.Precision.HIGHEST
    snapshot = following.astype(jnp.bfloat16)
    partial_coef = project(basis, snapshot) * dof_weight
    first_coef = lax.psum(partial_coef, ("gx", "gy", "gz"))
    first_resid = snapshot.astype(jnp.float32) - expand(basis, first_coef.astype(jnp.bfloat16))
    first_gram = lax.psum(local_gram(first_resid) * dof_weight, ("gx", "gy", "gz"))
    first_lower = jnp.linalg.cholesky(first_gram)
    first_q = apply_inverse(first_resid, first_lower)
    second_coef = lax.psum(
        project(basis, first_q.astype(jnp.bfloat16)) * dof_weight, ("gx", "gy", "gz")
    )
    second_resid = first_q - expand(basis, second_coef.astype(jnp.bfloat16))
    second_gram = lax.psum(local_gram(second_resid) * dof_weight, ("gx", "gy", "gz"))
    second_lower = jnp.linalg.cholesky(second_gram)
    modes = apply_inverse(second_resid, second_lower)
    factor = jnp.dot(first_lower, second_lower, precision=highest).T
    return (jnp.stack([first_coef, second_coef]), factor, modes)


def shards(basis, modal_now, modal_prev, material_ids, moduli, drive_mask, drive):
    devices_total = lax.axis_size("gx") * lax.axis_size("gy") * lax.axis_size("gz")
    dof_weight = 1.0 / (3.0 * basis.shape[0] * basis.shape[2] * basis.shape[3] * devices_total)
    current = expand(basis, modal_now)
    earlier = expand(basis, modal_prev)
    material_props = lookup(material_ids, moduli)
    port_mask = drive_mask.astype(jnp.float32)
    static = jnp.concatenate([material_props, port_mask], axis=0)
    wide_static = padded_2(static, (("gx", 1), ("gy", 2), ("gz", 3)), 2)
    props_wide = wide_static[:3]
    props_near = props_wide[:, 1:-1, 1:-1, 1:-1]
    inverse_mass = material_props[2]
    drive_field = drive[:, :, None, None, None]
    coefficient_list = []
    factor_list = []
    modes = current
    for step in range(STEPS):
        padded = padded_2(current, (("gx", 2), ("gy", 3), ("gz", 4)), 1)
        ramp_level = min(1.0, (step + 1) / ramp_steps)
        load_field = drive_field * port_mask[None] * ramp_level
        following = (
            2.0 * current
            - earlier
            + step_squared * inverse_mass * (load_field - stiffness(padded, props_near))
        )
        earlier = current
        current = following
        coefs, factor, modes = orthonormalize(following, basis, dof_weight)
        coefficient_list.append(coefs)
        factor_list.append(factor)
    return (current, modes, jnp.stack(coefficient_list), jnp.stack(factor_list))


def solution(mesh):
    in_specs = (
        P("gx", None, "gy", "gz", None),
        P(),
        P(),
        P("gx", "gy", "gz"),
        P(),
        P(None, "gx", "gy", "gz"),
        P(),
    )
    out_specs = (P(None, None, "gx", "gy", "gz"), P(None, None, "gx", "gy", "gz"), P(), P())
    return jax.shard_map(shards, mesh=mesh, in_specs=in_specs, out_specs=out_specs, check_vma=False)
```

profile of v0, /device:TPU:1, one launch (start us, length us, event | category | flops | bytes accessed | tf_op | source)
XLA Modules:
  0.0 537.8 jit_solution(7000948003984317785)
XLA Ops:
  2.5 4.0 collective-permute-start
  9.1 4.0 collective-permute-start.6
  14.7 3.7 collective-permute-done.7
  18.5 5.7 %collective-permute-start.8 = (f32[3,8,4,1,128]{4,1,3,2,0:T(8,128)S(1)}, f32[3,8,4,1,128]{4,1,3,2,0:T(8,128)S(1)}, u32[]{:S(2)}, u32[]{:S(2)}) collective-permute-start(f32[3,8,4,1,128]{4,1,3,2,0:T(8,128)S(1)} %get-tuple-element.78), channel_id=1, source_target_pairs={{0,8},{8,16},{16,24},{24,32},{32,40},{40,48},{48,56},{1,9},{9,17},... | collective-permute-start | bytes 147464 | tf_op jit(solution)/shard_map/ppermute | solution.py:16
  24.2 1.9 collective-permute-start.9
  26.2 3.4 collective-permute-done.9
  30.7 3.6 collective-permute-start.10
  35.7 3.8 copy.222
  39.5 2.2 collective-permute-start.2
  42.3 2.8 collective-permute-start.3
  45.9 2.0 collective-permute-done.11
  47.9 1.6 pad_maximum_fusion.1
  49.6 4.5 copy.221
  54.1 3.9 copy.223
  58.0 9.0 %pad_maximum_fusion = f32[11,6,12,128]{2,1,3,0:T(8,128)S(1)} fusion(f32[11,6,2,128]{2,1,3,0:T(8,128)} %copy.223, f32[11,6,8,128]{2,1,3,0:T(8,128)} %copy.222, f32[11,6,2,128]{2,1,3,0:T(8,128)} %copy.221), kind=kLoop, calls=%fused_computation | loop fusion | flops 202752 | bytes 811008 | tf_op jit(solution)/shard_map/concatenate | solution.py:20
  67.0 2.5 copy-done.1
  69.5 3.5 collective-permute-start.4
  75.3 4.2 copy.225
  86.2 3.2 collective-permute-start.12
  91.7 3.9 collective-permute-done.13
  95.6 5.9 %collective-permute-start.14 = (f32[3,8,4,1,128]{4,1,3,2,0:T(8,128)S(1)}, f32[3,8,4,1,128]{4,1,3,2,0:T(8,128)S(1)}, u32[]{:S(2)}, u32[]{:S(2)}) collective-permute-start(f32[3,8,4,1,128]{4,1,3,2,0:T(8,128)S(1)} %get-tuple-element.76), channel_id=1, source_target_pairs={{0,8},{8,16},{16,24},{24,32},{32,40},{40,48},{48,56},{1,9},{9,17},... | collective-permute-start | bytes 147464 | tf_op jit(solution)/shard_map/ppermute | solution.py:16
  101.6 1.9 collective-permute-start.15
  103.5 3.5 collective-permute-done.15
  107.2 4.9 collective-permute-start.16
  113.4 7.9 %collective-permute-done.16 = f32[3,8,4,10,1]{4,1,3,2,0:T(8,128)S(1)} collective-permute-done((f32[3,8,4,10,1]{4,1,3,2,0:T(8,128)S(1)}, f32[3,8,4,10,1]{4,1,3,2,0:T(8,128)S(1)}, u32[]{:S(2)}, u32[]{:S(2)}) %collective-permute-start.16) | collective-permute-done | bytes 3872 | tf_op jit(solution)/shard_map/ppermute | solution.py:16
  121.3 5.2 collective-permute-done.17
  127.7 2.9 collective-permute-start.18
  132.5 4.1 collective-permute-done.19
  136.7 5.3 collective-permute-start.20
  142.0 1.9 collective-permute-start.21
  143.9 3.5 collective-permute-done.21
  147.6 3.7 collective-permute-start.22
  152.8 7.7 %collective-permute-done.22 = f32[3,8,4,10,1]{4,1,3,2,0:T(8,128)S(1)} collective-permute-done((f32[3,8,4,10,1]{4,1,3,2,0:T(8,128)S(1)}, f32[3,8,4,10,1]{4,1,3,2,0:T(8,128)S(1)}, u32[]{:S(2)}, u32[]{:S(2)}) %collective-permute-start.22) | collective-permute-done | bytes 3872 | tf_op jit(solution)/shard_map/ppermute | solution.py:16
  160.5 4.1 collective-permute-done.23
  165.8 1.9 collective-permute-start.24
  169.6 4.1 collective-permute-done.25
  173.7 4.8 collective-permute-start.26
  178.5 1.9 collective-permute-start.27
  180.8 3.2 collective-permute-done.27
  184.2 4.6 collective-permute-start.28
  190.4 7.6 %collective-permute-done.28 = f32[3,8,4,10,1]{4,1,3,2,0:T(8,128)S(1)} collective-permute-done((f32[3,8,4,10,1]{4,1,3,2,0:T(8,128)S(1)}, f32[3,8,4,10,1]{4,1,3,2,0:T(8,128)S(1)}, u32[]{:S(2)}, u32[]{:S(2)}) %collective-permute-start.28) | collective-permute-done | bytes 3872 | tf_op jit(solution)/shard_map/ppermute | solution.py:16
  198.0 4.1 collective-permute-done.29
  203.5 73.7 %all-reduce.3 = (f32[128,8]{0,1:T(8,128)S(1)}, f32[128,8]{0,1:T(8,128)S(1)}, f32[128,8]{0,1:T(8,128)S(1)}, f32[128,8]{0,1:T(8,128)S(1)}) all-reduce(f32[128,8]{0,1:T(8,128)S(1)} %fusion.25, f32[128,8]{0,1:T(8,128)S(1)} %fusion.13, f32[128,8]{0,1:T(8,128)S(1)} %fusion.17, ...), channel_id=1, replica_groups=mesh['gx'=4,'gy'=8,'gz'=8] {'gx','gy','gz'}, use_global_device_ids=true, to_apply=%region_0.0 | all-reduce | flops 4096 | bytes 32768 | tf_op jit(solution)/shard_map/psum | solution.py:79
  281.4 73.0 %all-reduce.2 = (f32[8,8]{0,1:T(8,128)S(1)}, f32[8,8]{0,1:T(8,128)S(1)}, f32[8,8]{0,1:T(8,128)S(1)}, f32[8,8]{0,1:T(8,128)S(1)}) all-reduce(f32[8,8]{0,1:T(8,128)S(1)} %fusion.33, f32[8,8]{0,1:T(8,128)S(1)} %fusion.29, f32[8,8]{0,1:T(8,128)S(1)} %fusion.30, f32[8,8]{0,1:T(8,128)S(1)} %fusion.31), channel_id=1, replica_groups=mesh['gx'=4,'gy'=8,'gz'=8] {'gx','gy','gz'}, use_global_device_ids=true, to_apply=%region_1.0 | all-reduce | flops 256 | bytes 2048 | tf_op jit(solution)/shard_map/psum | solution.py:81
  368.8 74.7 %all-reduce.1 = (f32[128,8]{0,1:T(8,128)S(1)}, f32[128,8]{0,1:T(8,128)S(1)}, f32[128,8]{0,1:T(8,128)S(1)}, f32[128,8]{0,1:T(8,128)S(1)}) all-reduce(f32[128,8]{0,1:T(8,128)S(1)} %fusion.23, f32[128,8]{0,1:T(8,128)S(1)} %fusion.11, f32[128,8]{0,1:T(8,128)S(1)} %fusion.15, ...), channel_id=1, replica_groups=mesh['gx'=4,'gy'=8,'gz'=8] {'gx','gy','gz'}, use_global_device_ids=true, to_apply=%region_4.0 | all-reduce | flops 4096 | bytes 32768 | tf_op jit(solution)/shard_map/psum | solution.py:84
  447.7 73.6 %all-reduce = (f32[8,8]{0,1:T(8,128)S(1)}, f32[8,8]{0,1:T(8,128)S(1)}, f32[8,8]{0,1:T(8,128)S(1)}, f32[8,8]{0,1:T(8,128)S(1)}) all-reduce(f32[8,8]{0,1:T(8,128)S(1)} %fusion.32, f32[8,8]{0,1:T(8,128)S(1)} %fusion.26, f32[8,8]{0,1:T(8,128)S(1)} %fusion.27, f32[8,8]{0,1:T(8,128)S(1)} %fusion.28), channel_id=1, replica_groups=mesh['gx'=4,'gy'=8,'gz'=8] {'gx','gy','gz'}, use_global_device_ids=true, to_apply=%region_5.0 | all-reduce | flops 256 | bytes 2048 | tf_op jit(solution)/shard_map/psum | solution.py:88
  522.8 1.5 convolution_bitcast_fusion.16
  526.5 1.5 convolution_bitcast_fusion.19
  (192 shorter events, 70.2 us)
Async XLA Ops:
  0.6 7.2 %copy-start = (bf16[2,3,8,128,128]{4,3,2,1,0:T(8,128)(2,1)S(1)}, bf16[2,3,8,128,128]{4,3,2,1,0:T(8,128)(2,1)}, u32[]{:S(2)}) copy-start(bf16[2,3,8,128,128]{4,3,2,1,0:T(8,128)(2,1)} %param.10) | copy-start | bytes 4718596
  2.5 23.6 %collective-permute-start = (f32[11,2,8,128]{3,2,1,0:T(8,128)S(1)}, f32[11,2,8,128]{3,2,1,0:T(8,128)S(1)}, u32[]{:S(2)}, u32[]{:S(2)}) collective-permute-start(f32[11,2,8,128]{3,2,1,0:T(8,128)S(1)} %pad_maximum_fusion.10), channel_id=1, source_target_pairs={{0,64},{64,128},{128,192},{1,65},{65,129},{129,193},{2,66},{66,130... | collective-permute-start | bytes 270344 | tf_op jit(solution)/shard_map/ppermute | solution.py:16
  6.5 19.6 %collective-permute-start.1 = (f32[11,2,8,128]{3,2,1,0:T(8,128)S(1)}, f32[11,2,8,128]{3,2,1,0:T(8,128)S(1)}, u32[]{:S(2)}, u32[]{:S(2)}) collective-permute-start(f32[11,2,8,128]{3,2,1,0:T(8,128)S(1)} %pad_maximum_fusion.10), channel_id=1, source_target_pairs={{64,0},{128,64},{192,128},{65,1},{129,65},{193,129},{66,2},{130,66... | collective-permute-start | bytes 270344 | tf_op jit(solution)/shard_map/ppermute | solution.py:19
  9.1 5.6 %collective-permute-start.6 = (f32[3,8,1,8,128]{4,1,3,2,0:T(8,128)S(1)}, f32[3,8,1,8,128]{4,1,3,2,0:T(8,128)S(1)}, u32[]{:S(2)}, u32[]{:S(2)}) collective-permute-start(f32[3,8,1,8,128]{4,1,3,2,0:T(8,128)S(1)} %copy.383), channel_id=1, source_target_pairs={{0,64},{64,128},{128,192},{1,65},{65,129},{129,193},{2,66},{66,130... | collective-permute-start | bytes 294920 | tf_op jit(solution)/shard_map/ppermute | solution.py:16
  13.1 5.4 collective-permute-start.7
  18.5 7.7 %collective-permute-start.8 = (f32[3,8,4,1,128]{4,1,3,2,0:T(8,128)S(1)}, f32[3,8,4,1,128]{4,1,3,2,0:T(8,128)S(1)}, u32[]{:S(2)}, u32[]{:S(2)}) collective-permute-start(f32[3,8,4,1,128]{4,1,3,2,0:T(8,128)S(1)} %get-tuple-element.78), channel_id=1, source_target_pairs={{0,8},{8,16},{16,24},{24,32},{32,40},{40,48},{48,56},{1,9},{9,17},... | collective-permute-start | bytes 147464 | tf_op jit(solution)/shard_map/ppermute | solution.py:16
  24.2 5.4 %collective-permute-start.9 = (f32[3,8,4,1,128]{4,1,3,2,0:T(8,128)S(1)}, f32[3,8,4,1,128]{4,1,3,2,0:T(8,128)S(1)}, u32[]{:S(2)}, u32[]{:S(2)}) collective-permute-start(f32[3,8,4,1,128]{4,1,3,2,0:T(8,128)S(1)} %get-tuple-element.79), channel_id=1, source_target_pairs={{8,0},{16,8},{24,16},{32,24},{40,32},{48,40},{56,48},{9,1},{17,9},... | collective-permute-start | bytes 147464 | tf_op jit(solution)/shard_map/ppermute | solution.py:19
  30.7 14.4 %collective-permute-start.10 = (f32[3,8,4,10,1]{4,1,3,2,0:T(8,128)}, f32[3,8,4,10,1]{4,1,3,2,0:T(8,128)S(1)}, u32[]{:S(2)}, u32[]{:S(2)}) collective-permute-start(f32[3,8,4,10,1]{4,1,3,2,0:T(8,128)} %get-tuple-element.70), channel_id=1, source_target_pairs={{0,1},{1,2},{2,3},{3,4},{4,5},{5,6},{6,7},{8,9},{9,10},{10,11},{11... | collective-permute-start | bytes 11528 | tf_op jit(solution)/shard_map/ppermute | solution.py:16
  34.3 13.6 %collective-permute-start.11 = (f32[3,8,4,10,1]{4,1,3,2,0:T(8,128)}, f32[3,8,4,10,1]{4,1,3,2,0:T(8,128)}, u32[]{:S(2)}, u32[]{:S(2)}) collective-permute-start(f32[3,8,4,10,1]{4,1,3,2,0:T(8,128)} %get-tuple-element.71), channel_id=1, source_target_pairs={{1,0},{2,1},{3,2},{4,3},{5,4},{6,5},{7,6},{9,8},{10,9},{11,10},{12... | collective-permute-start | bytes 11528 | tf_op jit(solution)/shard_map/ppermute | solution.py:19
  39.5 10.1 %collective-permute-start.2 = (f32[11,6,2,128]{3,1,2,0:T(8,128)S(1)}, f32[11,6,2,128]{3,1,2,0:T(8,128)}, u32[]{:S(2)}, u32[]{:S(2)}) collective-permute-start(f32[11,6,2,128]{3,1,2,0:T(8,128)S(1)} %copy.326), channel_id=1, source_target_pairs={{0,8},{8,16},{16,24},{24,32},{32,40},{40,48},{48,56},{1,9},{9,17},... | collective-permute-start | bytes 202760 | tf_op jit(solution)/shard_map/ppermute | solution.py:16
  42.3 11.8 %collective-permute-start.3 = (f32[11,6,2,128]{3,1,2,0:T(8,128)}, f32[11,6,2,128]{3,1,2,0:T(8,128)S(1)}, u32[]{:S(2)}, u32[]{:S(2)}) collective-permute-start(f32[11,6,2,128]{3,1,2,0:T(8,128)} %copy.327), channel_id=1, source_target_pairs={{8,0},{16,8},{24,16},{32,24},{40,32},{48,40},{56,48},{9,1},{17,9},... | collective-permute-start | bytes 202760 | tf_op jit(solution)/shard_map/ppermute | solution.py:19
  45.1 0.8 copy-start.2
  67.0 2.5 copy-start.1
  69.5 10.0 %collective-permute-start.4 = (f32[11,6,12,2]{2,1,3,0:T(8,128)S(1)}, f32[11,6,12,2]{2,1,3,0:T(8,128)S(1)}, u32[]{:S(2)}, u32[]{:S(2)}) collective-permute-start(f32[11,6,12,2]{2,1,3,0:T(8,128)S(1)} %get-tuple-element.44), channel_id=1, source_target_pairs={{0,1},{1,2},{2,3},{3,4},{4,5},{5,6},{6,7},{8,9},{9,10},{10,11},{11... | collective-permute-start | bytes 19016 | tf_op jit(solution)/shard_map/ppermute | solution.py:16
  73.1 7.0 %collective-permute-start.5 = (f32[11,6,12,2]{2,1,3,0:T(8,128)S(1)}, f32[11,6,12,2]{2,1,3,0:T(8,128)S(1)}, u32[]{:S(2)}, u32[]{:S(2)}) collective-permute-start(f32[11,6,12,2]{2,1,3,0:T(8,128)S(1)} %get-tuple-element.45), channel_id=1, source_target_pairs={{1,0},{2,1},{3,2},{4,3},{5,4},{6,5},{7,6},{9,8},{10,9},{11,10},{12... | collective-permute-start | bytes 19016 | tf_op jit(solution)/shard_map/ppermute | solution.py:19
  81.4 4.2 copy-start.3
  81.4 4.3 copy-start.4
  86.2 5.6 %collective-permute-start.12 = (f32[3,8,1,8,128]{4,1,3,2,0:T(8,128)S(1)}, f32[3,8,1,8,128]{4,1,3,2,0:T(8,128)S(1)}, u32[]{:S(2)}, u32[]{:S(2)}) collective-permute-start(f32[3,8,1,8,128]{4,1,3,2,0:T(8,128)S(1)} %get-tuple-element.86), channel_id=1, source_target_pairs={{0,64},{64,128},{128,192},{1,65},{65,129},{129,193},{2,66},{66,130... | collective-permute-start | bytes 294920 | tf_op jit(solution)/shard_map/ppermute | solution.py:16
  89.4 6.2 %collective-permute-start.13 = (f32[3,8,1,8,128]{4,1,3,2,0:T(8,128)S(1)}, f32[3,8,1,8,128]{4,1,3,2,0:T(8,128)S(1)}, u32[]{:S(2)}, u32[]{:S(2)}) collective-permute-start(f32[3,8,1,8,128]{4,1,3,2,0:T(8,128)S(1)} %get-tuple-element.87), channel_id=1, source_target_pairs={{64,0},{128,64},{192,128},{65,1},{129,65},{193,129},{66,2},{130,66... | collective-permute-start | bytes 294920 | tf_op jit(solution)/shard_map/ppermute | solution.py:19
  95.6 7.9 %collective-permute-start.14 = (f32[3,8,4,1,128]{4,1,3,2,0:T(8,128)S(1)}, f32[3,8,4,1,128]{4,1,3,2,0:T(8,128)S(1)}, u32[]{:S(2)}, u32[]{:S(2)}) collective-permute-start(f32[3,8,4,1,128]{4,1,3,2,0:T(8,128)S(1)} %get-tuple-element.76), channel_id=1, source_target_pairs={{0,8},{8,16},{16,24},{24,32},{32,40},{40,48},{48,56},{1,9},{9,17},... | collective-permute-start | bytes 147464 | tf_op jit(solution)/shard_map/ppermute | solution.py:16
  101.6 5.4 %collective-permute-start.15 = (f32[3,8,4,1,128]{4,1,3,2,0:T(8,128)S(1)}, f32[3,8,4,1,128]{4,1,3,2,0:T(8,128)S(1)}, u32[]{:S(2)}, u32[]{:S(2)}) collective-permute-start(f32[3,8,4,1,128]{4,1,3,2,0:T(8,128)S(1)} %get-tuple-element.77), channel_id=1, source_target_pairs={{8,0},{16,8},{24,16},{32,24},{40,32},{48,40},{56,48},{9,1},{17,9},... | collective-permute-start | bytes 147464 | tf_op jit(solution)/shard_map/ppermute | solution.py:19
  107.2 14.1 %collective-permute-start.16 = (f32[3,8,4,10,1]{4,1,3,2,0:T(8,128)S(1)}, f32[3,8,4,10,1]{4,1,3,2,0:T(8,128)S(1)}, u32[]{:S(2)}, u32[]{:S(2)}) collective-permute-start(f32[3,8,4,10,1]{4,1,3,2,0:T(8,128)S(1)} %get-tuple-element.68), channel_id=1, source_target_pairs={{0,1},{1,2},{2,3},{3,4},{4,5},{5,6},{6,7},{8,9},{9,10},{10,11},{11... | collective-permute-start | bytes 11528 | tf_op jit(solution)/shard_map/ppermute | solution.py:16
  112.1 14.4 %collective-permute-start.17 = (f32[3,8,4,10,1]{4,1,3,2,0:T(8,128)S(1)}, f32[3,8,4,10,1]{4,1,3,2,0:T(8,128)S(1)}, u32[]{:S(2)}, u32[]{:S(2)}) collective-permute-start(f32[3,8,4,10,1]{4,1,3,2,0:T(8,128)S(1)} %get-tuple-element.69), channel_id=1, source_target_pairs={{1,0},{2,1},{3,2},{4,3},{5,4},{6,5},{7,6},{9,8},{10,9},{11,10},{12... | collective-permute-start | bytes 11528 | tf_op jit(solution)/shard_map/ppermute | solution.py:19
  127.7 4.8 collective-permute-start.18
  130.7 6.0 %collective-permute-start.19 = (f32[3,8,1,8,128]{4,1,3,2,0:T(8,128)S(1)}, f32[3,8,1,8,128]{4,1,3,2,0:T(8,128)S(1)}, u32[]{:S(2)}, u32[]{:S(2)}) collective-permute-start(f32[3,8,1,8,128]{4,1,3,2,0:T(8,128)S(1)} %copy.386), channel_id=1, source_target_pairs={{64,0},{128,64},{192,128},{65,1},{129,65},{193,129},{66,2},{130,66... | collective-permute-start | bytes 294920 | tf_op jit(solution)/shard_map/ppermute | solution.py:19
  136.7 7.2 %collective-permute-start.20 = (f32[3,8,4,1,128]{4,1,3,2,0:T(8,128)S(1)}, f32[3,8,4,1,128]{4,1,3,2,0:T(8,128)S(1)}, u32[]{:S(2)}, u32[]{:S(2)}) collective-permute-start(f32[3,8,4,1,128]{4,1,3,2,0:T(8,128)S(1)} %get-tuple-element.74), channel_id=1, source_target_pairs={{0,8},{8,16},{16,24},{24,32},{32,40},{40,48},{48,56},{1,9},{9,17},... | collective-permute-start | bytes 147464 | tf_op jit(solution)/shard_map/ppermute | solution.py:16
  142.0 5.4 %collective-permute-start.21 = (f32[3,8,4,1,128]{4,1,3,2,0:T(8,128)S(1)}, f32[3,8,4,1,128]{4,1,3,2,0:T(8,128)S(1)}, u32[]{:S(2)}, u32[]{:S(2)}) collective-permute-start(f32[3,8,4,1,128]{4,1,3,2,0:T(8,128)S(1)} %get-tuple-element.75), channel_id=1, source_target_pairs={{8,0},{16,8},{24,16},{32,24},{40,32},{48,40},{56,48},{9,1},{17,9},... | collective-permute-start | bytes 147464 | tf_op jit(solution)/shard_map/ppermute | solution.py:19
  147.6 12.9 %collective-permute-start.22 = (f32[3,8,4,10,1]{4,1,3,2,0:T(8,128)S(1)}, f32[3,8,4,10,1]{4,1,3,2,0:T(8,128)S(1)}, u32[]{:S(2)}, u32[]{:S(2)}) collective-permute-start(f32[3,8,4,10,1]{4,1,3,2,0:T(8,128)S(1)} %get-tuple-element.66), channel_id=1, source_target_pairs={{0,1},{1,2},{2,3},{3,4},{4,5},{5,6},{6,7},{8,9},{9,10},{10,11},{11... | collective-permute-start | bytes 11528 | tf_op jit(solution)/shard_map/ppermute | solution.py:16
  151.3 13.3 %collective-permute-start.23 = (f32[3,8,4,10,1]{4,1,3,2,0:T(8,128)S(1)}, f32[3,8,4,10,1]{4,1,3,2,0:T(8,128)S(1)}, u32[]{:S(2)}, u32[]{:S(2)}) collective-permute-start(f32[3,8,4,10,1]{4,1,3,2,0:T(8,128)S(1)} %get-tuple-element.67), channel_id=1, source_target_pairs={{1,0},{2,1},{3,2},{4,3},{5,4},{6,5},{7,6},{9,8},{10,9},{11,10},{12... | collective-permute-start | bytes 11528 | tf_op jit(solution)/shard_map/ppermute | solution.py:19
  165.8 3.8 collective-permute-start.24
  167.7 6.0 %collective-permute-start.25 = (f32[3,8,1,8,128]{4,1,3,2,0:T(8,128)S(1)}, f32[3,8,1,8,128]{4,1,3,2,0:T(8,128)S(1)}, u32[]{:S(2)}, u32[]{:S(2)}) collective-permute-start(f32[3,8,1,8,128]{4,1,3,2,0:T(8,128)S(1)} %get-tuple-element.83), channel_id=1, source_target_pairs={{64,0},{128,64},{192,128},{65,1},{129,65},{193,129},{66,2},{130,66... | collective-permute-start | bytes 294920 | tf_op jit(solution)/shard_map/ppermute | solution.py:19
  173.7 7.0 %collective-permute-start.26 = (f32[3,8,4,1,128]{4,1,3,2,0:T(8,128)S(1)}, f32[3,8,4,1,128]{4,1,3,2,0:T(8,128)S(1)}, u32[]{:S(2)}, u32[]{:S(2)}) collective-permute-start(f32[3,8,4,1,128]{4,1,3,2,0:T(8,128)S(1)} %get-tuple-element.72), channel_id=1, source_target_pairs={{0,8},{8,16},{16,24},{24,32},{32,40},{40,48},{48,56},{1,9},{9,17},... | collective-permute-start | bytes 147464 | tf_op jit(solution)/shard_map/ppermute | solution.py:16
  178.5 5.4 %collective-permute-start.27 = (f32[3,8,4,1,128]{4,1,3,2,0:T(8,128)S(1)}, f32[3,8,4,1,128]{4,1,3,2,0:T(8,128)S(1)}, u32[]{:S(2)}, u32[]{:S(2)}) collective-permute-start(f32[3,8,4,1,128]{4,1,3,2,0:T(8,128)S(1)} %get-tuple-element.73), channel_id=1, source_target_pairs={{8,0},{16,8},{24,16},{32,24},{40,32},{48,40},{56,48},{9,1},{17,9},... | collective-permute-start | bytes 147464 | tf_op jit(solution)/shard_map/ppermute | solution.py:19
  184.2 13.8 %collective-permute-start.28 = (f32[3,8,4,10,1]{4,1,3,2,0:T(8,128)S(1)}, f32[3,8,4,10,1]{4,1,3,2,0:T(8,128)S(1)}, u32[]{:S(2)}, u32[]{:S(2)}) collective-permute-start(f32[3,8,4,10,1]{4,1,3,2,0:T(8,128)S(1)} %get-tuple-element.64), channel_id=1, source_target_pairs={{0,1},{1,2},{2,3},{3,4},{4,5},{5,6},{6,7},{8,9},{9,10},{10,11},{11... | collective-permute-start | bytes 11528 | tf_op jit(solution)/shard_map/ppermute | solution.py:16
  188.8 13.3 %collective-permute-start.29 = (f32[3,8,4,10,1]{4,1,3,2,0:T(8,128)S(1)}, f32[3,8,4,10,1]{4,1,3,2,0:T(8,128)S(1)}, u32[]{:S(2)}, u32[]{:S(2)}) collective-permute-start(f32[3,8,4,10,1]{4,1,3,2,0:T(8,128)S(1)} %get-tuple-element.65), channel_id=1, source_target_pairs={{1,0},{2,1},{3,2},{4,3},{5,4},{6,5},{7,6},{9,8},{10,9},{11,10},{12... | collective-permute-start | bytes 11528 | tf_op jit(solution)/shard_map/ppermute | solution.py:19
where the time goes:
time: 540 us; the launch traced here: 538 us
  blocking collectives  295 us (55%)
  starting transfers between devices  83.7 us (16%)
  waiting for transfers between devices  70.1 us (13%)
  other arithmetic  38.1 us (7%)
  local copies, waits for them, and re-layouts  27.4 us (5%)
  matrix products  22 us (4%)
    psum x1, blocking collectives, orthonormalize(): lax.psum(project(basis, first_q.astype(jnp.bfloat16)) * dof_weight, ('gx'...  74.7 us
    psum x1, blocking collectives, orthonormalize(): first_coef = lax.psum(partial_coef, ('gx', 'gy', 'gz'))  73.7 us
    psum x1, blocking collectives, orthonormalize(): lax.psum(local_gram(second_resid) * dof_weight, ('gx', 'gy', 'gz'))  73.6 us
    psum x1, blocking collectives, orthonormalize(): lax.psum(local_gram(first_resid) * dof_weight, ('gx', 'gy', 'gz'))  73 us
    ppermute x15, starting transfers between devices, padded_2(): lax.ppermute(lax.slice_in_dim(block, block.shape[dim] - width, None, axis...  60.2 us
    ppermute x15, waiting for transfers between devices, padded_2(): lax.ppermute(lax.slice_in_dim(block, 0, width, axis=dim), axis, backward)  44.8 us
    ppermute x15, waiting for transfers between devices, padded_2(): lax.ppermute(lax.slice_in_dim(block, block.shape[dim] - width, None, axis...  25.3 us
    ppermute x15, starting transfers between devices, padded_2(): lax.ppermute(lax.slice_in_dim(block, 0, width, axis=dim), axis, backward)  23.6 us
  transfers between devices with their start and end apart: 30, of which 19 were waited for; matrix products, arithmetic and copies ran while one was open for 3% of the time, Pallas kernels for 0%

commit v1 on v0

--- a/solution.py
+++ b/solution.py
@@ -81,9 +81,9 @@
     first_gram = lax.psum(local_gram(first_resid) * dof_weight, ("gx", "gy", "gz"))
     first_lower = jnp.linalg.cholesky(first_gram)
     first_q = apply_inverse(first_resid, first_lower)
-    second_coef = lax.psum(
-        project(basis, first_q.astype(jnp.bfloat16)) * dof_weight, ("gx", "gy", "gz")
-    )
+    x = project(basis, first_q.astype(jnp.bfloat16)) * dof_weight
+    blocks = lax.all_gather(x, ("gx", "gy", "gz"), axis=0, tiled=False)
+    second_coef = blocks.sum(axis=0)
     second_resid = first_q - expand(basis, second_coef.astype(jnp.bfloat16))
     second_gram = lax.psum(local_gram(second_resid) * dof_weight, ("gx", "gy", "gz"))
     second_lower = jnp.linalg.cholesky(second_gram)

time: 540 us -> 884 us (1.64)
  waiting for transfers between devices: 70.1 us -> 464 us
  blocking collectives: 295 us -> 224 us
  between operations: 1.47 us -> 14.6 us
    all_gather x0 -> x4, waiting for transfers between devices: none -> 394 us  [orthonormalize(): blocks = lax.all_gather(x, ('gx', 'gy', 'gz'), axis=0, tiled=False)]
    psum x1 -> x0, blocking collectives: 74.7 us -> none  [orthonormalize(): lax.psum(project(basis, first_q.astype(jnp.bfloat16)) * dof_weight, ('gx'...]
  transfers between devices with their start and end apart: 30 -> 34, of which waited for: 19 -> 23; matrix products, arithmetic and copies ran while one was open for 3% -> 4% of each run, Pallas kernels for 0% -> 0%
where the time goes in v1:
time: 884 us; the launch traced here: 882 us
  waiting for transfers between devices  464 us (52%)
  blocking collectives  224 us (25%)
  starting transfers between devices  84 us (10%)
  other arithmetic  44 us (5%)
  local copies, waits for them, and re-layouts  27.4 us (3%)
  matrix products  24.3 us (3%)
  between operations  14.6 us (2%)
    all_gather x4, waiting for transfers between devices, orthonormalize(): blocks = lax.all_gather(x, ('gx', 'gy', 'gz'), axis=0, tiled=False)  394 us
    psum x1, blocking collectives, orthonormalize(): lax.psum(local_gram(second_resid) * dof_weight, ('gx', 'gy', 'gz'))  77 us
    psum x1, blocking collectives, orthonormalize(): first_coef = lax.psum(partial_coef, ('gx', 'gy', 'gz'))  73.7 us
    psum x1, blocking collectives, orthonormalize(): lax.psum(local_gram(first_resid) * dof_weight, ('gx', 'gy', 'gz'))  73 us
    ppermute x15, starting transfers between devices, padded_2(): lax.ppermute(lax.slice_in_dim(block, block.shape[dim] - width, None, axis...  60.1 us
    ppermute x15, waiting for transfers between devices, padded_2(): lax.ppermute(lax.slice_in_dim(block, 0, width, axis=dim), axis, backward)  44.9 us
    ppermute x15, waiting for transfers between devices, padded_2(): lax.ppermute(lax.slice_in_dim(block, block.shape[dim] - width, None, axis...  25.3 us
    ppermute x15, starting transfers between devices, padded_2(): lax.ppermute(lax.slice_in_dim(block, 0, width, axis=dim), axis, backward)  23.6 us
  transfers between devices with their start and end apart: 34, of which 23 were waited for; matrix products, arithmetic and copies ran while one was open for 4% of the time, Pallas kernels for 0%

profile of v1, /device:TPU:1, one launch (start us, length us, event | category | flops | bytes accessed | tf_op | source)
XLA Modules:
  0.0 882.0 jit_solution(14951427481508531063)
XLA Ops:
  9.1 4.0 collective-permute-start
  15.7 4.0 collective-permute-start.6
  21.3 3.7 collective-permute-done.7
  25.1 5.7 collective-permute-start.8
  30.7 1.9 collective-permute-start.9
  32.7 3.4 collective-permute-done.9
  37.3 3.6 collective-permute-start.10
  42.2 3.8 copy.222
  46.0 2.2 collective-permute-start.2
  48.9 2.8 collective-permute-start.3
  52.5 2.0 collective-permute-done.11
  56.1 4.5 copy.221
  60.7 3.9 copy.223
  64.6 9.0 %pad_maximum_fusion = f32[11,6,12,128]{2,1,3,0:T(8,128)S(1)} fusion(f32[11,6,2,128]{2,1,3,0:T(8,128)} %copy.223, f32[11,6,8,128]{2,1,3,0:T(8,128)} %copy.222, f32[11,6,2,128]{2,1,3,0:T(8,128)} %copy.221), kind=kLoop, calls=%fused_computation | loop fusion | flops 202752 | bytes 811008 | tf_op jit(solution)/shard_map/concatenate | solution.py:20
  73.6 2.5 copy-done.1
  76.1 3.5 collective-permute-start.4
  81.8 4.2 copy.225
  92.8 3.2 collective-permute-start.12
  98.3 3.9 collective-permute-done.13
  102.2 5.9 collective-permute-start.14
  108.2 1.9 collective-permute-start.15
  110.1 3.5 collective-permute-done.15
  113.8 4.9 collective-permute-start.16
  120.0 7.9 collective-permute-done.16
  127.9 5.2 collective-permute-done.17
  134.3 2.9 collective-permute-start.18
  139.1 4.1 collective-permute-done.19
  143.2 5.3 collective-permute-start.20
  148.5 1.9 collective-permute-start.21
  150.5 3.5 collective-permute-done.21
  154.2 3.7 collective-permute-start.22
  159.3 7.7 collective-permute-done.22
  167.0 4.1 collective-permute-done.23
  172.4 1.9 collective-permute-start.24
  176.2 4.1 collective-permute-done.25
  180.3 4.8 collective-permute-start.26
  185.1 1.9 collective-permute-start.27
  187.3 3.2 collective-permute-done.27
  190.7 4.6 collective-permute-start.28
  196.9 7.6 collective-permute-done.28
  204.5 4.1 collective-permute-done.29
  210.1 73.7 %all-reduce.2 = (f32[128,8]{0,1:T(8,128)S(1)}, f32[128,8]{0,1:T(8,128)S(1)}, f32[128,8]{0,1:T(8,128)S(1)}, f32[128,8]{0,1:T(8,128)S(1)}) all-reduce(f32[128,8]{0,1:T(8,128)S(1)} %fusion.25, f32[128,8]{0,1:T(8,128)S(1)} %fusion.13, f32[128,8]{0,1:T(8,128)S(1)} %fusion.17, ...), channel_id=1, replica_groups=mesh['gx'=4,'gy'=8,'gz'=8] {'gx','gy','gz'}, use_global_device_ids=true, to_apply=%region_0.0 | all-reduce | flops 4096 | bytes 32768 | tf_op jit(solution)/shard_map/psum | solution.py:79
  288.0 73.0 %all-reduce.1 = (f32[8,8]{0,1:T(8,128)S(1)}, f32[8,8]{0,1:T(8,128)S(1)}, f32[8,8]{0,1:T(8,128)S(1)}, f32[8,8]{0,1:T(8,128)S(1)}) all-reduce(f32[8,8]{0,1:T(8,128)S(1)} %fusion.33, f32[8,8]{0,1:T(8,128)S(1)} %fusion.29, f32[8,8]{0,1:T(8,128)S(1)} %fusion.30, f32[8,8]{0,1:T(8,128)S(1)} %fusion.31), channel_id=1, replica_groups=mesh['gx'=4,'gy'=8,'gz'=8] {'gx','gy','gz'}, use_global_device_ids=true, to_apply=%region_1.0 | all-reduce | flops 256 | bytes 2048 | tf_op jit(solution)/shard_map/psum | solution.py:81
  379.0 85.5 %all-gather.11.cloned.1.call-done = f32[32768,8]{0,1:T(8,128)} async-done(((f32[128,8]{0,1:T(8,128)}), f32[32768,8]{0,1:T(8,128)}) %all-gather.11.cloned.1.call-update) | async-done | bytes 1048592 | tf_op jit(solution)/shard_map/all_gather | solution.py:85
  466.0 103.8 %all-gather.13.cloned.1.call-done = f32[32768,8]{0,1:T(8,128)} async-done(((f32[128,8]{0,1:T(8,128)}), f32[32768,8]{0,1:T(8,128)}) %all-gather.13.cloned.1.call-update) | async-done | bytes 1048592 | tf_op jit(solution)/shard_map/all_gather | solution.py:85
  571.3 103.8 %all-gather.15.cloned.1.call-done = f32[32768,8]{0,1:T(8,128)} async-done(((f32[128,8]{0,1:T(8,128)}), f32[32768,8]{0,1:T(8,128)}) %all-gather.15.cloned.1.call-update) | async-done | bytes 1048592 | tf_op jit(solution)/shard_map/all_gather | solution.py:85
  679.8 100.5 %all-gather.9.cloned.1.call-done = f32[32768,8]{0,1:T(8,128)} async-done(((f32[128,8]{0,1:T(8,128)}), f32[32768,8]{0,1:T(8,128)}) %all-gather.9.cloned.1.call-update) | async-done | bytes 1048592 | tf_op jit(solution)/shard_map/all_gather | solution.py:85
  782.9 77.0 %all-reduce = (f32[8,8]{0,1:T(8,128)S(1)}, f32[8,8]{0,1:T(8,128)S(1)}, f32[8,8]{0,1:T(8,128)S(1)}, f32[8,8]{0,1:T(8,128)S(1)}) all-reduce(f32[8,8]{0,1:T(8,128)S(1)} %fusion.32, f32[8,8]{0,1:T(8,128)S(1)} %fusion.26, f32[8,8]{0,1:T(8,128)S(1)} %fusion.27, f32[8,8]{0,1:T(8,128)S(1)} %fusion.28), channel_id=1, replica_groups=mesh['gx'=4,'gy'=8,'gz'=8] {'gx','gy','gz'}, use_global_device_ids=true, to_apply=%region_5.0 | all-reduce | flops 256 | bytes 2048 | tf_op jit(solution)/shard_map/psum | solution.py:88
  (207 shorter events, 83.4 us)
Async XLA Ops:
  7.2 7.3 copy-start
  7.2 457.3 %all-gather.11.cloned.1.call-start = ((), (), s32[]{:S(2)}) async-start(), calls=%async_computation.1 | async-start | bytes 1052672 | tf_op jit(solution)/shard_map/all_gather | solution.py:85
  9.1 23.6 %collective-permute-start = (f32[11,2,8,128]{3,2,1,0:T(8,128)S(1)}, f32[11,2,8,128]{3,2,1,0:T(8,128)S(1)}, u32[]{:S(2)}, u32[]{:S(2)}) collective-permute-start(f32[11,2,8,128]{3,2,1,0:T(8,128)S(1)} %pad_maximum_fusion.10), channel_id=1, source_target_pairs={{0,64},{64,128},{128,192},{1,65},{65,129},{129,193},{2,66},{66,130... | collective-permute-start | bytes 270344 | tf_op jit(solution)/shard_map/ppermute | solution.py:16
  13.1 19.6 %collective-permute-start.1 = (f32[11,2,8,128]{3,2,1,0:T(8,128)S(1)}, f32[11,2,8,128]{3,2,1,0:T(8,128)S(1)}, u32[]{:S(2)}, u32[]{:S(2)}) collective-permute-start(f32[11,2,8,128]{3,2,1,0:T(8,128)S(1)} %pad_maximum_fusion.10), channel_id=1, source_target_pairs={{64,0},{128,64},{192,128},{65,1},{129,65},{193,129},{66,2},{130,66... | collective-permute-start | bytes 270344 | tf_op jit(solution)/shard_map/ppermute | solution.py:19
  15.7 5.6 collective-permute-start.6
  19.7 5.4 collective-permute-start.7
  25.1 7.7 collective-permute-start.8
  30.7 5.4 collective-permute-start.9
  37.3 14.4 %collective-permute-start.10 = (f32[3,8,4,10,1]{4,1,3,2,0:T(8,128)}, f32[3,8,4,10,1]{4,1,3,2,0:T(8,128)S(1)}, u32[]{:S(2)}, u32[]{:S(2)}) collective-permute-start(f32[3,8,4,10,1]{4,1,3,2,0:T(8,128)} %get-tuple-element.66), channel_id=1, source_target_pairs={{0,1},{1,2},{2,3},{3,4},{4,5},{5,6},{6,7},{8,9},{9,10},{10,11},{11... | collective-permute-start | bytes 11528 | tf_op jit(solution)/shard_map/ppermute | solution.py:16
  40.9 13.6 %collective-permute-start.11 = (f32[3,8,4,10,1]{4,1,3,2,0:T(8,128)}, f32[3,8,4,10,1]{4,1,3,2,0:T(8,128)}, u32[]{:S(2)}, u32[]{:S(2)}) collective-permute-start(f32[3,8,4,10,1]{4,1,3,2,0:T(8,128)} %get-tuple-element.67), channel_id=1, source_target_pairs={{1,0},{2,1},{3,2},{4,3},{5,4},{6,5},{7,6},{9,8},{10,9},{11,10},{12... | collective-permute-start | bytes 11528 | tf_op jit(solution)/shard_map/ppermute | solution.py:19
  46.0 10.1 %collective-permute-start.2 = (f32[11,6,2,128]{3,1,2,0:T(8,128)S(1)}, f32[11,6,2,128]{3,1,2,0:T(8,128)}, u32[]{:S(2)}, u32[]{:S(2)}) collective-permute-start(f32[11,6,2,128]{3,1,2,0:T(8,128)S(1)} %copy.326), channel_id=1, source_target_pairs={{0,8},{8,16},{16,24},{24,32},{32,40},{40,48},{48,56},{1,9},{9,17},... | collective-permute-start | bytes 202760 | tf_op jit(solution)/shard_map/ppermute | solution.py:16
  48.9 11.8 %collective-permute-start.3 = (f32[11,6,2,128]{3,1,2,0:T(8,128)}, f32[11,6,2,128]{3,1,2,0:T(8,128)S(1)}, u32[]{:S(2)}, u32[]{:S(2)}) collective-permute-start(f32[11,6,2,128]{3,1,2,0:T(8,128)} %copy.327), channel_id=1, source_target_pairs={{8,0},{16,8},{24,16},{32,24},{40,32},{48,40},{56,48},{9,1},{17,9},... | collective-permute-start | bytes 202760 | tf_op jit(solution)/shard_map/ppermute | solution.py:19
  51.7 0.8 copy-start.2
  73.6 2.5 copy-start.1
  76.1 10.0 %collective-permute-start.4 = (f32[11,6,12,2]{2,1,3,0:T(8,128)S(1)}, f32[11,6,12,2]{2,1,3,0:T(8,128)S(1)}, u32[]{:S(2)}, u32[]{:S(2)}) collective-permute-start(f32[11,6,12,2]{2,1,3,0:T(8,128)S(1)} %get-tuple-element.40), channel_id=1, source_target_pairs={{0,1},{1,2},{2,3},{3,4},{4,5},{5,6},{6,7},{8,9},{9,10},{10,11},{11... | collective-permute-start | bytes 19016 | tf_op jit(solution)/shard_map/ppermute | solution.py:16
  79.6 7.0 collective-permute-start.5
  87.9 4.3 copy-start.3
  87.9 4.3 copy-start.4
  92.8 5.6 collective-permute-start.12
  96.0 6.3 collective-permute-start.13
  102.2 7.9 collective-permute-start.14
  108.2 5.4 collective-permute-start.15
  113.8 14.1 %collective-permute-start.16 = (f32[3,8,4,10,1]{4,1,3,2,0:T(8,128)S(1)}, f32[3,8,4,10,1]{4,1,3,2,0:T(8,128)S(1)}, u32[]{:S(2)}, u32[]{:S(2)}) collective-permute-start(f32[3,8,4,10,1]{4,1,3,2,0:T(8,128)S(1)} %get-tuple-element.64), channel_id=1, source_target_pairs={{0,1},{1,2},{2,3},{3,4},{4,5},{5,6},{6,7},{8,9},{9,10},{10,11},{11... | collective-permute-start | bytes 11528 | tf_op jit(solution)/shard_map/ppermute | solution.py:16
  118.7 14.4 %collective-permute-start.17 = (f32[3,8,4,10,1]{4,1,3,2,0:T(8,128)S(1)}, f32[3,8,4,10,1]{4,1,3,2,0:T(8,128)S(1)}, u32[]{:S(2)}, u32[]{:S(2)}) collective-permute-start(f32[3,8,4,10,1]{4,1,3,2,0:T(8,128)S(1)} %get-tuple-element.65), channel_id=1, source_target_pairs={{1,0},{2,1},{3,2},{4,3},{5,4},{6,5},{7,6},{9,8},{10,9},{11,10},{12... | collective-permute-start | bytes 11528 | tf_op jit(solution)/shard_map/ppermute | solution.py:19
  134.3 4.8 collective-permute-start.18
  137.2 6.0 collective-permute-start.19
  143.2 7.2 collective-permute-start.20
  148.5 5.4 collective-permute-start.21
  154.2 12.9 %collective-permute-start.22 = (f32[3,8,4,10,1]{4,1,3,2,0:T(8,128)S(1)}, f32[3,8,4,10,1]{4,1,3,2,0:T(8,128)S(1)}, u32[]{:S(2)}, u32[]{:S(2)}) collective-permute-start(f32[3,8,4,10,1]{4,1,3,2,0:T(8,128)S(1)} %get-tuple-element.62), channel_id=1, source_target_pairs={{0,1},{1,2},{2,3},{3,4},{4,5},{5,6},{6,7},{8,9},{9,10},{10,11},{11... | collective-permute-start | bytes 11528 | tf_op jit(solution)/shard_map/ppermute | solution.py:16
  157.9 13.3 %collective-permute-start.23 = (f32[3,8,4,10,1]{4,1,3,2,0:T(8,128)S(1)}, f32[3,8,4,10,1]{4,1,3,2,0:T(8,128)S(1)}, u32[]{:S(2)}, u32[]{:S(2)}) collective-permute-start(f32[3,8,4,10,1]{4,1,3,2,0:T(8,128)S(1)} %get-tuple-element.63), channel_id=1, source_target_pairs={{1,0},{2,1},{3,2},{4,3},{5,4},{6,5},{7,6},{9,8},{10,9},{11,10},{12... | collective-permute-start | bytes 11528 | tf_op jit(solution)/shard_map/ppermute | solution.py:19
  172.4 3.8 collective-permute-start.24
  174.3 6.0 collective-permute-start.25
  180.3 7.0 collective-permute-start.26
  185.1 5.4 collective-permute-start.27
  190.7 13.8 %collective-permute-start.28 = (f32[3,8,4,10,1]{4,1,3,2,0:T(8,128)S(1)}, f32[3,8,4,10,1]{4,1,3,2,0:T(8,128)S(1)}, u32[]{:S(2)}, u32[]{:S(2)}) collective-permute-start(f32[3,8,4,10,1]{4,1,3,2,0:T(8,128)S(1)} %get-tuple-element.60), channel_id=1, source_target_pairs={{0,1},{1,2},{2,3},{3,4},{4,5},{5,6},{6,7},{8,9},{9,10},{10,11},{11... | collective-permute-start | bytes 11528 | tf_op jit(solution)/shard_map/ppermute | solution.py:16
  195.3 13.3 %collective-permute-start.29 = (f32[3,8,4,10,1]{4,1,3,2,0:T(8,128)S(1)}, f32[3,8,4,10,1]{4,1,3,2,0:T(8,128)S(1)}, u32[]{:S(2)}, u32[]{:S(2)}) collective-permute-start(f32[3,8,4,10,1]{4,1,3,2,0:T(8,128)S(1)} %get-tuple-element.61), channel_id=1, source_target_pairs={{1,0},{2,1},{3,2},{4,3},{5,4},{6,5},{7,6},{9,8},{10,9},{11,10},{12... | collective-permute-start | bytes 11528 | tf_op jit(solution)/shard_map/ppermute | solution.py:19
  365.2 204.7 %all-gather.13.cloned.1.call-start = ((), (), s32[]{:S(2)}) async-start(), calls=%async_computation.2 | async-start | bytes 1052672 | tf_op jit(solution)/shard_map/all_gather | solution.py:85
  369.6 305.6 %all-gather.15.cloned.1.call-start = ((), (), s32[]{:S(2)}) async-start(), calls=%async_computation.3 | async-start | bytes 1052672 | tf_op jit(solution)/shard_map/all_gather | solution.py:85
  373.7 406.6 %all-gather.9.cloned.1.call-start = ((), (), s32[]{:S(2)}) async-start(), calls=%async_computation | async-start | bytes 1052672 | tf_op jit(solution)/shard_map/all_gather | solution.py:85
Sparse Core Ops, SparseCore 0:
  365.3 99.1 all-gather.10
  468.8 100.9 all-gather.12
  574.1 100.9 all-gather.14
  679.3 100.9 all-gather.8
